TPU v7x, 128 devices: a whole 4x4x4 slice. The times are simulated.
128 devices in a mesh: det: 16 (over z_lo, x, core), strip: 8 (over y, z_hi).
Axes of the slice: x: 4, y: 4, z: 4 (z_hi: 2, z_lo: 2; z = z_hi * 2 + z_lo), core: 2. Of those that a mesh axis runs over, the one named last changes fastest.
Arguments:
- science: float32 [16, 256, 4096], P('det', 'strip'), may hold values from -17 to 17
- template: float32 [16, 256, 4096], P(None, 'strip', 'det'), may hold values from -8 to 8
- row_taps: float32 [12, 21], replicated, may hold values from -1.25 to 1.25
- col_taps: float32 [12, 21], replicated, may hold values from -1.25 to 1.25
- stamp_rows: int32 [16, 32], P('det'), may hold values from 17 to 238
- stamp_cols: int32 [16, 32], P('det'), may hold values from 17 to 4078
Outputs:
- difference: float32 [16, 256, 4096], P('det', 'strip')
- kernel_coeffs: float32 [16, 37], P('det')
All inputs are finite; a program needn't handle non-finite values.
Results may differ from a plain program's by a relative error of at most 0.0003.
Values sent between devices are 32-bit elements; how exact they have to be, the bound alone decides.
A program may use at most 128 MiB of HBM per device.

v0:
```python
import jax
import jax.numpy as jnp
from jax import lax
from jax.sharding import PartitionSpec as P

NB = 12
KS = 21
HS = 17
KH = 10
NU = 37
RIDGE_WEIGHT = 1.0
HIGHEST_MODE = lax.Precision.HIGHEST
LANE_WIDTH = 128


def padded_2(block, sides, width):
    for axis, dim in sides:
        count = lax.axis_size(axis)
        forward = [(i, i + 1) for i in range(count - 1)]
        backward = [(target, source) for source, target in forward]
        low = lax.ppermute(
            lax.slice_in_dim(block, block.shape[dim] - width, None, axis=dim), axis, forward
        )
        high = lax.ppermute(lax.slice_in_dim(block, 0, width, axis=dim), axis, backward)
        block = jnp.concatenate([low, block, high], axis=dim)
    return block


def column_tables(col_taps):
    offset = jnp.arange(2 * LANE_WIDTH)[:, None] - jnp.arange(LANE_WIDTH)[None, :]
    onehot = (offset[None] == jnp.arange(KS)[:, None, None]).astype(jnp.float32)
    whole = jnp.einsum("bv,vij->bij", col_taps, onehot, precision=HIGHEST_MODE)
    return (whole[:, :LANE_WIDTH, :], whole[:, LANE_WIDTH:, :])


def row_table(row_taps, row_count):
    offset = jnp.arange(row_count + 2 * KH)[None, :] - jnp.arange(row_count)[:, None]
    onehot = (offset[None] == jnp.arange(KS)[:, None, None]).astype(jnp.float32)
    return jnp.einsum("bv,vyk->byk", row_taps, onehot, precision=HIGHEST_MODE)


def correlate(framed, main_tab, next_tab, row_tab):
    depth, col_count = framed.shape
    col_blocks = col_count // LANE_WIDTH
    padded = jnp.pad(framed, ((0, 0), (KH, LANE_WIDTH - KH)))
    central = padded[:, :col_count].reshape(depth, col_blocks, LANE_WIDTH)
    following = padded[:, LANE_WIDTH : col_count + LANE_WIDTH].reshape(
        depth, col_blocks, LANE_WIDTH
    )
    across = jnp.einsum("rki,bij->brkj", central, main_tab, precision=HIGHEST_MODE)
    across = across + jnp.einsum("rki,bij->brkj", following, next_tab, precision=HIGHEST_MODE)
    across = across.reshape(NB, depth, col_count)
    return jnp.einsum("byk,bkc->byc", row_tab, across, precision=HIGHEST_MODE)


def apply_model(responses, coeffs, y_coord, x_coord):
    base_part = jnp.tensordot(coeffs[:NB], responses, axes=1, precision=HIGHEST_MODE)
    x_part = jnp.tensordot(coeffs[NB : 2 * NB], responses, axes=1, precision=HIGHEST_MODE)
    y_part = jnp.tensordot(coeffs[2 * NB : 3 * NB], responses, axes=1, precision=HIGHEST_MODE)
    return base_part + x_coord * x_part + y_coord * y_part + coeffs[NU - 1]


def local(science, template, row_taps, col_taps, stamp_rows, stamp_cols):
    det_count, row_count, col_count = science.shape
    moved = lax.all_to_all(template, "det", split_axis=0, concat_axis=2, tiled=True)
    framed = padded_2(moved, (("strip", 1),), KH)
    total_rows = row_count * lax.axis_size("strip")
    first_global = lax.axis_index("strip") * row_count
    global_rows = first_global + jnp.arange(row_count, dtype=jnp.int32)
    y_coord = (2.0 * global_rows.astype(jnp.float32) / total_rows - 1.0)[:, None]
    col_index = jnp.arange(col_count, dtype=jnp.int32)
    x_coord = (2.0 * col_index.astype(jnp.float32) / col_count - 1.0)[None, :]
    main_tab, next_tab = column_tables(col_taps)
    row_tab = row_table(row_taps, row_count)
    y_flat = jnp.broadcast_to(y_coord, (row_count, col_count)).reshape(1, -1)
    x_flat = jnp.broadcast_to(x_coord, (row_count, col_count)).reshape(1, -1)
    unity = jnp.ones((1, row_count * col_count), jnp.float32)
    responses = correlate(framed[0], main_tab, next_tab, row_tab)
    observed = science[0]
    row_hits = (jnp.abs(global_rows[:, None] - stamp_rows[0][None, :]) <= HS).astype(jnp.float32)
    col_hits = (jnp.abs(stamp_cols[0][:, None] - col_index[None, :]) <= HS).astype(jnp.float32)
    weight = jnp.dot(
        row_hits, col_hits, precision=HIGHEST_MODE, preferred_element_type=jnp.float32
    ).reshape(1, -1)
    flat = responses.reshape(NB, -1)
    feats = jnp.concatenate([flat, flat * x_flat, flat * y_flat, unity], axis=0)
    weighted = feats * weight
    normal = jnp.einsum("ip,jp->ij", weighted, feats, precision=HIGHEST_MODE)
    target = jnp.einsum("ip,p->i", weighted, observed.reshape(-1), precision=HIGHEST_MODE)
    normal, target = lax.psum((normal, target), "strip")
    normal = normal + RIDGE_WEIGHT * jnp.eye(NU, dtype=jnp.float32)
    factor = jnp.linalg.cholesky(normal)
    coeffs = jax.scipy.linalg.cho_solve((factor, True), target)
    differences = [observed - apply_model(responses, coeffs, y_coord, x_coord)]
    solutions = [coeffs]
    return (jnp.stack(differences), jnp.stack(solutions))


def solution(mesh):
    return jax.shard_map(
        local,
        mesh=mesh,
        in_specs=(
            P("det", "strip", None),
            P(None, "strip", "det"),
            P(),
            P(),
            P("det", None),
            P("det", None),
        ),
        out_specs=(P("det", "strip", None), P("det", None)),
        check_vma=False,
    )
```

profile of v0, /device:TPU:0, one launch (start us, length us, event | category | flops | bytes accessed | tf_op | source)
XLA Modules:
  0.0 230.5 jit_solution(16646424460032151319)
XLA Ops:
  0.7 6.1 %all-to-all-start = ((f32[16,32,256]{2,1,0:T(8,128)}), f32[16,32,256]{2,1,0:T(8,128)}, u32[]{:S(2)}, u32[]{:S(2)}) async-start(f32[16,32,256]{2,1,0:T(8,128)} %param.7), calls=%async_computation | async-start | bytes 1048576 | tf_op jit(solution)/shard_map/all_to_all | solution.py:65
  7.2 1.0 convolution_bitcast_fusion
  8.2 0.9 copy.36
  9.1 2.4 %copy.37 = f32[1,1,32,4096]{3,1,2,0:T(1,128)} copy(f32[1,1,32,4096]{3,2,1,0:T(8,128)} %bitcast.123) | data formatting | bytes 1048576
  11.4 1.4 fusion.15
  13.1 4.5 %all-to-all-done = f32[16,32,256]{2,1,0:T(8,128)} async-done(((f32[16,32,256]{2,1,0:T(8,128)}), f32[16,32,256]{2,1,0:T(8,128)}, u32[]{:S(2)}, u32[]{:S(2)}) %all-to-all-start) | async-done | bytes 524320 | tf_op jit(solution)/shard_map/all_to_all | solution.py:65
  17.6 1.1 copy.30
  18.7 5.5 %collective-permute-start = (f32[1,10,4096]{2,1,0:T(8,128)S(1)}, f32[1,10,4096]{2,1,0:T(8,128)S(1)}, u32[]{:S(2)}, u32[]{:S(2)}) collective-permute-start(f32[1,10,4096]{2,1,0:T(8,128)S(1)} %get-tuple-element.10), channel_id=1, source_target_pairs={{0,1},{1,2},{2,3},{3,4},{4,5},{5,6},{6,7},{8,9},{9,10},{10,11},{11... | collective-permute-start | bytes 491528 | tf_op jit(solution)/shard_map/ppermute | solution.py:21
  24.3 1.5 collective-permute-start.1
  26.0 8.6 %collective-permute-done = f32[1,10,4096]{2,1,0:T(8,128)S(1)} collective-permute-done((f32[1,10,4096]{2,1,0:T(8,128)S(1)}, f32[1,10,4096]{2,1,0:T(8,128)S(1)}, u32[]{:S(2)}, u32[]{:S(2)}) %collective-permute-start) | collective-permute-done | bytes 163872 | tf_op jit(solution)/shard_map/ppermute | solution.py:21
  35.8 9.2 %fusion.21 = f32[12,128,52,32]{1,2,3,0:T(8,128)S(1)} fusion(f32[52,32,128]{2,1,0:T(8,128)S(1)} %slice.63, f32[12,128,128,1]{2,0,1,3:T(8,128)S(1)} %get-tuple-element.7), kind=kOutput, calls=%fused_computation.29 | convolution fusion | flops 3925868544 | bytes 11862016 | tf_op jit(solution)/shard_map/rki,bij->brkj/dot_general | solution.py:50
  45.0 10.5 %add_bitcast_fusion = f32[12,52,32,128]{3,1,2,0:T(8,128)S(1)} fusion(f32[12,128,52,32]{1,2,3,0:T(8,128)S(1)} %fusion.21, f32[52,32,128]{2,1,0:T(8,128)S(1)} %slice.64, f32[12,128,128,1]{2,0,1,3:T(8,128)S(1)} %get-tuple-element.6), kind=kOutput, calls=%fused_computation.5 | convolution fusion | flops 3928424448 | bytes 22085632 | tf_op jit(solution)/shard_map/rki,bij->brkj/dot_general | solution.py:51
  55.5 5.5 %copy.16 = f32[12,52,32,128]{3,2,1,0:T(8,128)} copy(f32[12,52,32,128]{3,1,2,0:T(8,128)S(1)} %add_bitcast_fusion) | data formatting | bytes 20447232 | tf_op jit(solution)/shard_map/add | solution.py:51
  61.0 10.2 %reshape.85 = f32[12,52,4096]{2,1,0:T(8,128)} reshape(f32[12,52,32,128]{3,2,1,0:T(8,128)} %copy.16) | data formatting | bytes 20447232 | tf_op jit(solution)/shard_map/reshape | solution.py:52
  71.2 9.3 %fusion.36 = f32[12,32,4096]{2,1,0:T(8,128)S(1)} fusion(f32[12,52,4096]{2,1,0:T(8,128)} %reshape.85, f32[32,52,12]{1,2,0:T(8,128)S(1)} %fusion.32), kind=kOutput, calls=%fused_computation.52 | convolution fusion | flops 981467136 | bytes 16594944 | tf_op jit(solution)/shard_map/byk,bkc->byc/dot_general | solution.py:53
  80.5 2.7 %copy-done.2 = f32[12,32,4096]{2,1,0:T(8,128)} copy-done((f32[12,32,4096]{2,1,0:T(8,128)}, f32[12,32,4096]{2,1,0:T(8,128)S(1)}, u32[]{:S(2)}) %copy-start.2) | copy-done | bytes 6291480
  83.2 0.9 pad.12
  84.1 4.9 %copy.33 = f32[2,8,32,4096]{3,1,2,0:T(8,128)S(1)} copy(f32[2,8,32,4096]{3,2,1,0:T(8,128)S(1)} %bitcast.116) | data formatting | bytes 16777216
  89.0 6.6 %broadcast_multiply_fusion.1 = (f32[12,131072]{1,0:T(8,128)}, f32[12,131072]{1,0:T(8,128)}) fusion(f32[12,131072]{1,0:T(8,128)S(1)} %bitcast.113, f32[131072]{0:T(1024)S(1)} %bitcast.125, f32[131072]{0:T(1024)S(1)} %bitcast.124), kind=kLoop, calls=%fused_computation.17 | loop fusion | flops 3145728 | bytes 19922944 | tf_op jit(solution)/shard_map/mul | solution.py:86
  95.7 1.6 copy-done.3
  97.3 26.7 %fusion.2 = f32[37,37]{1,0:T(8,128)S(1)} fusion(f32[12,131072]{1,0:T(8,128)} %get-tuple-element.5, f32[12,131072]{1,0:T(8,128)} %get-tuple-element.4, f32[12,131072]{1,0:T(8,128)} %bitcast.114, f32[37]{0:T(128)S(1)} %pad.8.clone, f32[131072]{0:T(1024)S(1)} %bitcast.126), kind=kOutput, calls=%fused_computation.2 | convolution fusion | flops 2187198464 | bytes 19404280 | tf_op jit(solution)/shard_map/ip,jp->ij/dot_general | solution.py:88
  124.0 21.7 %fusion.17 = f32[37]{0:T(128)S(1)} fusion(f32[131072,1]{0,1:T(1,128)S(1)} %bitcast.128, f32[12,131072]{1,0:T(8,128)} %get-tuple-element.5, f32[12,131072]{1,0:T(8,128)} %get-tuple-element.4, f32[12,131072]{1,0:T(8,128)} %bitcast.115, f32[37]{0:T(128)S(1)} %pad.8.clone, f32[131072]{0:T(1024)S(1)} %bitcast.127), kind=kOutput, calls=%fused_computation.23 | convolution fusion | flops 77594624 | bytes 19923240 | tf_op jit(solution)/shard_map/ip,p->i/dot_general | solution.py:89
  145.7 41.4 %all-reduce.1 = (f32[37,37]{1,0:T(8,128)S(1)}, f32[37]{0:T(128)S(1)}) all-reduce(f32[37,37]{1,0:T(8,128)S(1)} %fusion.2, f32[37]{0:T(128)S(1)} %fusion.17), channel_id=1, replica_groups=mesh['det'=16,'strip'=8] {'strip'}, use_global_device_ids=true, to_apply=%region_0.1 | all-reduce | flops 1406 | bytes 11248 | tf_op jit(solution)/shard_map/psum | solution.py:90
  187.2 3.4 %cholesky.17 = f32[37,37]{1,0:T(8,128)S(1)} custom-call(f32[37,37]{1,0:T(8,128)S(1)} %fusion.43), custom_call_target="Cholesky" | custom-call | tf_op jit(solution)/shard_map/jit(cholesky)/cholesky | solution.py:92
  190.6 0.6 compare_reduce_fusion
  191.2 0.7 fusion.39
  191.9 2.8 %custom-call.10 = f32[1,37,37]{1,2,0:T(8,128)S(1)} custom-call(f32[1,37,37]{2,1,0:T(8,128)S(1)} %fusion.39), custom_call_target="InvertDiagBlocksLowerTriangular" | custom-call | tf_op jit(solution)/shard_map/jit(_cho_solve)/triangular_solve | solution.py:93
  195.0 11.3 %fusion.12 = f32[1,32,4096]{2,0,1:T(1,128)S(1)} fusion(f32[12,32,4096]{2,1,0:T(8,128)} %copy-done.2, f32[37]{0:T(128)S(1)} %bitcast.129), kind=kOutput, calls=%fused_computation.14 | convolution fusion | flops 18874368 | bytes 6815892 | tf_op jit(solution)/shard_map/dot_general | solution.py:57
  206.4 11.4 %fusion.10 = f32[1,32,4096]{2,0,1:T(1,128)S(1)} fusion(f32[12,32,4096]{2,1,0:T(8,128)} %copy-done.2, f32[37]{0:T(128)S(1)} %bitcast.130), kind=kOutput, calls=%fused_computation.12 | convolution fusion | flops 18874368 | bytes 6815892 | tf_op jit(solution)/shard_map/dot_general | solution.py:58
  217.8 9.3 %fusion.8 = f32[1,32,4096]{2,0,1:T(1,128)S(1)} fusion(f32[12,32,4096]{2,1,0:T(8,128)S(1)} %bitcast.112, f32[37]{0:T(128)S(1)} %bitcast.131), kind=kOutput, calls=%fused_computation.10 | convolution fusion | flops 18874368 | bytes 6815892 | tf_op jit(solution)/shard_map/dot_general | solution.py:59
  227.1 0.6 slice.58
  227.7 2.5 %fusion.30 = f32[1,32,4096]{2,1,0:T(8,128)} fusion(f32[1,32,4096]{2,1,0:T(8,128)S(1)} %copy-done.4, f32[1,32,4096]{2,0,1:T(1,128)S(1)} %fusion.8, f32[1,32,4096]{2,0,1:T(1,128)S(1)} %fusion.10, f32[1,32,4096]{2,0,1:T(1,128)S(1)} %fusion.12, f32[]{:T(128)} %bitcast.29, f32[32]{0:T(128)S(1)} %multiply_add_fusion.1, f32[4096]{0:T(1024)S(1)} %multiply_add_fusion), kind=kLoop, calls=%fused_computation.41 | loop fusion | flops 786432 | bytes 2637956 | tf_op jit(solution)/shard_map/stack | solution.py:96
  (48 shorter events, 2.5 us)
Async XLA Ops:
  0.6 10.8 %copy-start = (f32[12,21]{1,0:T(8,128)S(1)}, f32[12,21]{1,0:T(8,128)}, u32[]{:S(2)}) copy-start(f32[12,21]{1,0:T(8,128)} %param.9) | copy-start | bytes 3028
  0.6 25.1 %copy-start.8 = (f32[12,21]{1,0:T(8,128)S(1)}, f32[12,21]{1,0:T(8,128)}, u32[]{:S(2)}) copy-start(f32[12,21]{1,0:T(8,128)} %param.8) | copy-start | bytes 3028
  0.7 17.0 %all-to-all-start = ((f32[16,32,256]{2,1,0:T(8,128)}), f32[16,32,256]{2,1,0:T(8,128)}, u32[]{:S(2)}, u32[]{:S(2)}) async-start(f32[16,32,256]{2,1,0:T(8,128)} %param.7), calls=%async_computation | async-start | bytes 1048576 | tf_op jit(solution)/shard_map/all_to_all | solution.py:65
  18.7 15.9 %collective-permute-start = (f32[1,10,4096]{2,1,0:T(8,128)S(1)}, f32[1,10,4096]{2,1,0:T(8,128)S(1)}, u32[]{:S(2)}, u32[]{:S(2)}) collective-permute-start(f32[1,10,4096]{2,1,0:T(8,128)S(1)} %get-tuple-element.10), channel_id=1, source_target_pairs={{0,1},{1,2},{2,3},{3,4},{4,5},{5,6},{6,7},{8,9},{9,10},{10,11},{11... | collective-permute-start | bytes 491528 | tf_op jit(solution)/shard_map/ppermute | solution.py:21
  24.3 10.4 %collective-permute-start.1 = (f32[1,10,4096]{2,1,0:T(8,128)S(1)}, f32[1,10,4096]{2,1,0:T(8,128)S(1)}, u32[]{:S(2)}, u32[]{:S(2)}) collective-permute-start(f32[1,10,4096]{2,1,0:T(8,128)S(1)} %get-tuple-element.11), channel_id=1, source_target_pairs={{1,0},{2,1},{3,2},{4,3},{5,4},{6,5},{7,6},{9,8},{10,9},{11,10},{12... | collective-permute-start | bytes 491528 | tf_op jit(solution)/shard_map/ppermute | solution.py:24
  80.5 2.7 %copy-start.2 = (f32[12,32,4096]{2,1,0:T(8,128)}, f32[12,32,4096]{2,1,0:T(8,128)S(1)}, u32[]{:S(2)}) copy-start(f32[12,32,4096]{2,1,0:T(8,128)S(1)} %fusion.36) | copy-start | bytes 18874372
  89.0 8.3 %copy-start.3 = (f32[2,8,32,4096]{3,1,2,0:T(8,128)}, f32[2,8,32,4096]{3,1,2,0:T(8,128)S(1)}, u32[]{:S(2)}) copy-start(f32[2,8,32,4096]{3,1,2,0:T(8,128)S(1)} %copy.33) | copy-start | bytes 25165828
  89.0 8.3 %copy-start.5 = (f32[4,32,8,128]{3,1,2,0:T(8,128)S(1)}, f32[4,32,8,128]{3,1,2,0:T(8,128)}, u32[]{:S(2)}) copy-start(f32[4,32,8,128]{3,1,2,0:T(8,128)} %copy.36) | copy-start | bytes 1572868
  97.3 26.7 %copy-start.6 = (f32[1,1,32,4096]{3,1,2,0:T(1,128)S(1)}, f32[1,1,32,4096]{3,1,2,0:T(1,128)}, u32[]{:S(2)}) copy-start(f32[1,1,32,4096]{3,1,2,0:T(1,128)} %copy.37) | copy-start | bytes 1572868
  195.0 32.1 %copy-start.7 = (f32[1,37]{1,0:T(1,128)}, f32[1,37]{1,0:T(1,128)S(1)}, u32[]{:S(2)}) copy-start(f32[1,37]{1,0:T(1,128)S(1)} %fusion.40) | copy-start | bytes 448
  195.0 22.8 %slice-start = ((s8[6291456]{0:T(1024)(128)(4,1)}), s8[4194304]{0:T(1024)(128)(4,1)S(1)}, s32[]{:S(2)}) async-start(s8[6291456]{0:T(1024)(128)(4,1)} %bitcast.111), calls=%async_computation.1 | async-start | bytes 8388608
  195.0 35.2 %copy-start.1 = (f32[12,21]{1,0:T(8,128)S(1)}, f32[12,21]{1,0:T(8,128)}, u32[]{:S(2)}) copy-start(f32[12,21]{1,0:T(8,128)} %param.9) | copy-start | bytes 3028
  206.4 11.4 %slice-start.1 = ((s8[6291456]{0:T(1024)(128)(4,1)}), s8[2097152]{0:T(1024)(128)(4,1)S(1)}, s32[]{:S(2)}) async-start(s8[6291456]{0:T(1024)(128)(4,1)} %bitcast.111), calls=%async_computation.2 | async-start | bytes 4194304
  206.4 21.3 %copy-start.4 = (f32[1,32,4096]{2,1,0:T(8,128)S(1)}, f32[1,32,4096]{2,1,0:T(8,128)}, u32[]{:S(2)}) copy-start(f32[1,32,4096]{2,1,0:T(8,128)} %param.6) | copy-start | bytes 1572868
where the time goes:
time: 234 us; the launch traced here: 230 us
  matrix products  112 us (48%)
  blocking collectives  41.4 us (18%)
  local copies, waits for them, and re-layouts  32.4 us (14%)
  other arithmetic  16.9 us (7%)
  waiting for transfers between devices  13.1 us (6%)
  starting transfers between devices  13 us (6%)
    psum x1, blocking collectives, local(): normal, target = lax.psum((normal, target), 'strip')  41.4 us
    dot_general x1, matrix products, local(): normal = jnp.einsum('ip,jp->ij', weighted, feats, precision=HIGHEST_MODE)  26.7 us
    dot_general x1, matrix products, local(): jnp.einsum('ip,p->i', weighted, observed.reshape(-1), precision=HIGHEST_M...  21.7 us
    unnamed x32, local copies, waits for them, and re-layouts  14 us
    dot_general x1, matrix products, apply_model(): jnp.tensordot(coeffs[NB:2 * NB], responses, axes=1, precision=HIGHEST_MODE)  11.4 us
    dot_general x1, matrix products, apply_model(): jnp.tensordot(coeffs[:NB], responses, axes=1, precision=HIGHEST_MODE)  11.3 us
    dot_general x1, matrix products, correlate(): jnp.einsum('rki,bij->brkj', following, next_tab, precision=HIGHEST_MODE)  10.5 us
    reshape x1, local copies, waits for them, and re-layouts, correlate(): across = across.reshape(NB, depth, col_count)  10.2 us
  transfers between devices with their start and end apart: 3, of which 2 were waited for; matrix products, arithmetic and copies ran while one was open for 3% of the time, Pallas kernels for 0%

commit v1 on v0

--- a/solution.py
+++ b/solution.py
@@ -62,7 +62,10 @@
 
 def local(science, template, row_taps, col_taps, stamp_rows, stamp_cols):
     det_count, row_count, col_count = science.shape
-    moved = lax.all_to_all(template, "det", split_axis=0, concat_axis=2, tiled=True)
+    moved = jnp.concatenate(
+        lax.all_to_all(jnp.stack(jnp.split(template, lax.axis_size("det"), axis=0)), "det", 0, 0),
+        axis=2,
+    )
     framed = padded_2(moved, (("strip", 1),), KH)
     total_rows = row_count * lax.axis_size("strip")
     first_global = lax.axis_index("strip") * row_count

time: 234 us -> 257 us (1.098)
  local copies, waits for them, and re-layouts: 32.4 us -> 54.4 us
    unnamed x32 -> x47, local copies, waits for them, and re-layouts: 14 us -> 34.7 us
where the time goes in v1:
time: 257 us; the launch traced here: 252 us
  matrix products  112 us (44%)
  local copies, waits for them, and re-layouts  54.4 us (21%)
  blocking collectives  41.4 us (16%)
  other arithmetic  16.9 us (7%)
  waiting for transfers between devices  13.1 us (5%)
  starting transfers between devices  12.9 us (5%)
    psum x1, blocking collectives, local(): normal, target = lax.psum((normal, target), 'strip')  41.4 us
    unnamed x47, local copies, waits for them, and re-layouts  34.7 us
    dot_general x1, matrix products, local(): normal = jnp.einsum('ip,jp->ij', weighted, feats, precision=HIGHEST_MODE)  26.7 us
    dot_general x1, matrix products, local(): jnp.einsum('ip,p->i', weighted, observed.reshape(-1), precision=HIGHEST_M...  21.7 us
    dot_general x1, matrix products, apply_model(): jnp.tensordot(coeffs[NB:2 * NB], responses, axes=1, precision=HIGHEST_MODE)  11.4 us
    dot_general x1, matrix products, apply_model(): jnp.tensordot(coeffs[:NB], responses, axes=1, precision=HIGHEST_MODE)  11.3 us
    dot_general x1, matrix products, correlate(): jnp.einsum('rki,bij->brkj', following, next_tab, precision=HIGHEST_MODE)  10.5 us
    reshape x1, local copies, waits for them, and re-layouts, correlate(): across = across.reshape(NB, depth, col_count)  10.2 us
  transfers between devices with their start and end apart: 3, of which 2 were waited for; matrix products, arithmetic and copies ran while one was open for 3% of the time, Pallas kernels for 0%

profile of v1, /device:TPU:0, one launch (start us, length us, event | category | flops | bytes accessed | tf_op | source)
XLA Modules:
  0.0 252.3 jit_solution(15528039854793234216)
XLA Ops:
  0.7 1.4 constant_dynamic-update-slice_fusion.15
  2.0 1.4 constant_dynamic-update-slice_fusion.14
  3.4 1.4 constant_dynamic-update-slice_fusion.13
  7.5 1.4 constant_dynamic-update-slice_fusion.10
  10.3 1.4 constant_dynamic-update-slice_fusion.8
  13.0 1.4 constant_dynamic-update-slice_fusion.6
  15.8 1.4 constant_dynamic-update-slice_fusion.4
  22.7 5.9 %all-to-all-start = ((f32[16,1,32,256]{3,2,1,0:T(8,128)}), f32[16,1,32,256]{3,2,1,0:T(8,128)}, u32[]{:S(2)}, u32[]{:S(2)}) async-start(f32[16,1,32,256]{3,2,1,0:T(8,128)} %constant_dynamic-update-slice_fusion), calls=%async_computation | async-start | bytes 1048576 | tf_op jit(solution)/shard_map/all_to_all | solution.py:66
  30.9 2.4 copy.37
  33.3 1.4 fusion.15
  35.0 4.5 %all-to-all-done = f32[16,1,32,256]{3,2,1,0:T(8,128)} async-done(((f32[16,1,32,256]{3,2,1,0:T(8,128)}), f32[16,1,32,256]{3,2,1,0:T(8,128)}, u32[]{:S(2)}, u32[]{:S(2)}) %all-to-all-start) | async-done | bytes 524320 | tf_op jit(solution)/shard_map/all_to_all | solution.py:66
  40.6 5.5 %collective-permute-start = (f32[1,10,4096]{2,1,0:T(8,128)S(1)}, f32[1,10,4096]{2,1,0:T(8,128)S(1)}, u32[]{:S(2)}, u32[]{:S(2)}) collective-permute-start(f32[1,10,4096]{2,1,0:T(8,128)S(1)} %get-tuple-element.10), channel_id=1, source_target_pairs={{0,1},{1,2},{2,3},{3,4},{4,5},{5,6},{6,7},{8,9},{9,10},{10,11},{11... | collective-permute-start | bytes 491528 | tf_op jit(solution)/shard_map/ppermute | solution.py:21
  46.1 1.5 collective-permute-start.1
  47.9 8.6 %collective-permute-done = f32[1,10,4096]{2,1,0:T(8,128)S(1)} collective-permute-done((f32[1,10,4096]{2,1,0:T(8,128)S(1)}, f32[1,10,4096]{2,1,0:T(8,128)S(1)}, u32[]{:S(2)}, u32[]{:S(2)}) %collective-permute-start) | collective-permute-done | bytes 163872 | tf_op jit(solution)/shard_map/ppermute | solution.py:21
  57.6 9.2 %fusion.21 = f32[12,128,52,32]{1,2,3,0:T(8,128)S(1)} fusion(f32[52,32,128]{2,1,0:T(8,128)S(1)} %slice.63, f32[12,128,128,1]{2,0,1,3:T(8,128)S(1)} %get-tuple-element.7), kind=kOutput, calls=%fused_computation.29 | convolution fusion | flops 3925868544 | bytes 11862016 | tf_op jit(solution)/shard_map/rki,bij->brkj/dot_general | solution.py:50
  66.8 10.5 %add_bitcast_fusion = f32[12,52,32,128]{3,1,2,0:T(8,128)S(1)} fusion(f32[12,128,52,32]{1,2,3,0:T(8,128)S(1)} %fusion.21, f32[52,32,128]{2,1,0:T(8,128)S(1)} %slice.64, f32[12,128,128,1]{2,0,1,3:T(8,128)S(1)} %get-tuple-element.6), kind=kOutput, calls=%fused_computation.5 | convolution fusion | flops 3928424448 | bytes 22085632 | tf_op jit(solution)/shard_map/rki,bij->brkj/dot_general | solution.py:51
  77.4 5.5 %copy.16 = f32[12,52,32,128]{3,2,1,0:T(8,128)} copy(f32[12,52,32,128]{3,1,2,0:T(8,128)S(1)} %add_bitcast_fusion) | data formatting | bytes 20447232 | tf_op jit(solution)/shard_map/add | solution.py:51
  82.9 10.2 %reshape.93 = f32[12,52,4096]{2,1,0:T(8,128)} reshape(f32[12,52,32,128]{3,2,1,0:T(8,128)} %copy.16) | data formatting | bytes 20447232 | tf_op jit(solution)/shard_map/reshape | solution.py:52
  93.1 9.3 %fusion.36 = f32[12,32,4096]{2,1,0:T(8,128)S(1)} fusion(f32[12,52,4096]{2,1,0:T(8,128)} %reshape.93, f32[32,52,12]{1,2,0:T(8,128)S(1)} %fusion.32), kind=kOutput, calls=%fused_computation.52 | convolution fusion | flops 981467136 | bytes 16594944 | tf_op jit(solution)/shard_map/byk,bkc->byc/dot_general | solution.py:53
  102.4 2.7 %copy-done.2 = f32[12,32,4096]{2,1,0:T(8,128)} copy-done((f32[12,32,4096]{2,1,0:T(8,128)}, f32[12,32,4096]{2,1,0:T(8,128)S(1)}, u32[]{:S(2)}) %copy-start.2) | copy-done | bytes 6291480
  106.0 4.9 %copy.33 = f32[2,8,32,4096]{3,1,2,0:T(8,128)S(1)} copy(f32[2,8,32,4096]{3,2,1,0:T(8,128)S(1)} %bitcast.146) | data formatting | bytes 16777216
  110.9 6.6 %broadcast_multiply_fusion.1 = (f32[12,131072]{1,0:T(8,128)}, f32[12,131072]{1,0:T(8,128)}) fusion(f32[12,131072]{1,0:T(8,128)S(1)} %bitcast.143, f32[131072]{0:T(1024)S(1)} %bitcast.155, f32[131072]{0:T(1024)S(1)} %bitcast.154), kind=kLoop, calls=%fused_computation.17 | loop fusion | flops 3145728 | bytes 19922944 | tf_op jit(solution)/shard_map/mul | solution.py:89
  117.5 1.6 copy-done.3
  119.1 26.7 %fusion.2 = f32[37,37]{1,0:T(8,128)S(1)} fusion(f32[12,131072]{1,0:T(8,128)} %get-tuple-element.5, f32[12,131072]{1,0:T(8,128)} %get-tuple-element.4, f32[12,131072]{1,0:T(8,128)} %bitcast.144, f32[37]{0:T(128)S(1)} %pad.8.clone, f32[131072]{0:T(1024)S(1)} %bitcast.156), kind=kOutput, calls=%fused_computation.2 | convolution fusion | flops 2187198464 | bytes 19404280 | tf_op jit(solution)/shard_map/ip,jp->ij/dot_general | solution.py:91
  145.9 21.7 %fusion.17 = f32[37]{0:T(128)S(1)} fusion(f32[131072,1]{0,1:T(1,128)S(1)} %bitcast.158, f32[12,131072]{1,0:T(8,128)} %get-tuple-element.5, f32[12,131072]{1,0:T(8,128)} %get-tuple-element.4, f32[12,131072]{1,0:T(8,128)} %bitcast.145, f32[37]{0:T(128)S(1)} %pad.8.clone, f32[131072]{0:T(1024)S(1)} %bitcast.157), kind=kOutput, calls=%fused_computation.23 | convolution fusion | flops 77594624 | bytes 19923240 | tf_op jit(solution)/shard_map/ip,p->i/dot_general | solution.py:92
  167.5 41.4 %all-reduce.1 = (f32[37,37]{1,0:T(8,128)S(1)}, f32[37]{0:T(128)S(1)}) all-reduce(f32[37,37]{1,0:T(8,128)S(1)} %fusion.2, f32[37]{0:T(128)S(1)} %fusion.17), channel_id=1, replica_groups=mesh['det'=16,'strip'=8] {'strip'}, use_global_device_ids=true, to_apply=%region_0.1 | all-reduce | flops 1406 | bytes 11248 | tf_op jit(solution)/shard_map/psum | solution.py:93
  209.0 3.4 %cholesky.17 = f32[37,37]{1,0:T(8,128)S(1)} custom-call(f32[37,37]{1,0:T(8,128)S(1)} %fusion.43), custom_call_target="Cholesky" | custom-call | tf_op jit(solution)/shard_map/jit(cholesky)/cholesky | solution.py:95
  213.7 2.8 %custom-call.10 = f32[1,37,37]{1,2,0:T(8,128)S(1)} custom-call(f32[1,37,37]{2,1,0:T(8,128)S(1)} %fusion.39), custom_call_target="InvertDiagBlocksLowerTriangular" | custom-call | tf_op jit(solution)/shard_map/jit(_cho_solve)/triangular_solve | solution.py:96
  216.9 11.3 %fusion.12 = f32[1,32,4096]{2,0,1:T(1,128)S(1)} fusion(f32[12,32,4096]{2,1,0:T(8,128)} %copy-done.2, f32[37]{0:T(128)S(1)} %bitcast.159), kind=kOutput, calls=%fused_computation.14 | convolution fusion | flops 18874368 | bytes 6815892 | tf_op jit(solution)/shard_map/dot_general | solution.py:57
  228.3 11.4 %fusion.10 = f32[1,32,4096]{2,0,1:T(1,128)S(1)} fusion(f32[12,32,4096]{2,1,0:T(8,128)} %copy-done.2, f32[37]{0:T(128)S(1)} %bitcast.160), kind=kOutput, calls=%fused_computation.12 | convolution fusion | flops 18874368 | bytes 6815892 | tf_op jit(solution)/shard_map/dot_general | solution.py:58
  239.6 9.3 %fusion.8 = f32[1,32,4096]{2,0,1:T(1,128)S(1)} fusion(f32[12,32,4096]{2,1,0:T(8,128)S(1)} %bitcast.142, f32[37]{0:T(128)S(1)} %bitcast.161), kind=kOutput, calls=%fused_computation.10 | convolution fusion | flops 18874368 | bytes 6815892 | tf_op jit(solution)/shard_map/dot_general | solution.py:59
  249.5 2.5 %fusion.30 = f32[1,32,4096]{2,1,0:T(8,128)} fusion(f32[1,32,4096]{2,1,0:T(8,128)S(1)} %copy-done.4, f32[1,32,4096]{2,0,1:T(1,128)S(1)} %fusion.8, f32[1,32,4096]{2,0,1:T(1,128)S(1)} %fusion.10, f32[1,32,4096]{2,0,1:T(1,128)S(1)} %fusion.12, f32[]{:T(128)} %bitcast.44, f32[32]{0:T(128)S(1)} %multiply_add_fusion.1, f32[4096]{0:T(1024)S(1)} %multiply_add_fusion), kind=kLoop, calls=%fused_computation.41 | loop fusion | flops 786432 | bytes 2637956 | tf_op jit(solution)/shard_map/stack | solution.py:99
  (64 shorter events, 20.7 us)
Async XLA Ops:
  0.6 32.7 %copy-start = (f32[12,21]{1,0:T(8,128)S(1)}, f32[12,21]{1,0:T(8,128)}, u32[]{:S(2)}) copy-start(f32[12,21]{1,0:T(8,128)} %param.9) | copy-start | bytes 3028
  0.6 46.9 %copy-start.8 = (f32[12,21]{1,0:T(8,128)S(1)}, f32[12,21]{1,0:T(8,128)}, u32[]{:S(2)}) copy-start(f32[12,21]{1,0:T(8,128)} %param.8) | copy-start | bytes 3028
  22.7 16.8 %all-to-all-start = ((f32[16,1,32,256]{3,2,1,0:T(8,128)}), f32[16,1,32,256]{3,2,1,0:T(8,128)}, u32[]{:S(2)}, u32[]{:S(2)}) async-start(f32[16,1,32,256]{3,2,1,0:T(8,128)} %constant_dynamic-update-slice_fusion), calls=%async_computation | async-start | bytes 1048576 | tf_op jit(solution)/shard_map/all_to_all | solution.py:66
  40.6 15.9 %collective-permute-start = (f32[1,10,4096]{2,1,0:T(8,128)S(1)}, f32[1,10,4096]{2,1,0:T(8,128)S(1)}, u32[]{:S(2)}, u32[]{:S(2)}) collective-permute-start(f32[1,10,4096]{2,1,0:T(8,128)S(1)} %get-tuple-element.10), channel_id=1, source_target_pairs={{0,1},{1,2},{2,3},{3,4},{4,5},{5,6},{6,7},{8,9},{9,10},{10,11},{11... | collective-permute-start | bytes 491528 | tf_op jit(solution)/shard_map/ppermute | solution.py:21
  46.1 10.4 %collective-permute-start.1 = (f32[1,10,4096]{2,1,0:T(8,128)S(1)}, f32[1,10,4096]{2,1,0:T(8,128)S(1)}, u32[]{:S(2)}, u32[]{:S(2)}) collective-permute-start(f32[1,10,4096]{2,1,0:T(8,128)S(1)} %get-tuple-element.11), channel_id=1, source_target_pairs={{1,0},{2,1},{3,2},{4,3},{5,4},{6,5},{7,6},{9,8},{10,9},{11,10},{12... | collective-permute-start | bytes 491528 | tf_op jit(solution)/shard_map/ppermute | solution.py:24
  102.4 2.7 %copy-start.2 = (f32[12,32,4096]{2,1,0:T(8,128)}, f32[12,32,4096]{2,1,0:T(8,128)S(1)}, u32[]{:S(2)}) copy-start(f32[12,32,4096]{2,1,0:T(8,128)S(1)} %fusion.36) | copy-start | bytes 18874372
  110.9 8.3 %copy-start.3 = (f32[2,8,32,4096]{3,1,2,0:T(8,128)}, f32[2,8,32,4096]{3,1,2,0:T(8,128)S(1)}, u32[]{:S(2)}) copy-start(f32[2,8,32,4096]{3,1,2,0:T(8,128)S(1)} %copy.33) | copy-start | bytes 25165828
  110.9 8.3 %copy-start.5 = (f32[4,32,8,128]{3,1,2,0:T(8,128)S(1)}, f32[4,32,8,128]{3,1,2,0:T(8,128)}, u32[]{:S(2)}) copy-start(f32[4,32,8,128]{3,1,2,0:T(8,128)} %copy.36) | copy-start | bytes 1572868
  119.1 26.7 %copy-start.6 = (f32[1,1,32,4096]{3,1,2,0:T(1,128)S(1)}, f32[1,1,32,4096]{3,1,2,0:T(1,128)}, u32[]{:S(2)}) copy-start(f32[1,1,32,4096]{3,1,2,0:T(1,128)} %copy.37) | copy-start | bytes 1572868
  216.9 32.1 %copy-start.7 = (f32[1,37]{1,0:T(1,128)}, f32[1,37]{1,0:T(1,128)S(1)}, u32[]{:S(2)}) copy-start(f32[1,37]{1,0:T(1,128)S(1)} %fusion.40) | copy-start | bytes 448
  216.9 22.8 %slice-start = ((s8[6291456]{0:T(1024)(128)(4,1)}), s8[4194304]{0:T(1024)(128)(4,1)S(1)}, s32[]{:S(2)}) async-start(s8[6291456]{0:T(1024)(128)(4,1)} %bitcast.141), calls=%async_computation.1 | async-start | bytes 8388608
  216.9 35.2 %copy-start.1 = (f32[12,21]{1,0:T(8,128)S(1)}, f32[12,21]{1,0:T(8,128)}, u32[]{:S(2)}) copy-start(f32[12,21]{1,0:T(8,128)} %param.9) | copy-start | bytes 3028
  228.2 11.4 %slice-start.1 = ((s8[6291456]{0:T(1024)(128)(4,1)}), s8[2097152]{0:T(1024)(128)(4,1)S(1)}, s32[]{:S(2)}) async-start(s8[6291456]{0:T(1024)(128)(4,1)} %bitcast.141), calls=%async_computation.2 | async-start | bytes 4194304
  228.2 21.3 %copy-start.4 = (f32[1,32,4096]{2,1,0:T(8,128)S(1)}, f32[1,32,4096]{2,1,0:T(8,128)}, u32[]{:S(2)}) copy-start(f32[1,32,4096]{2,1,0:T(8,128)} %param.6) | copy-start | bytes 1572868
